TPU v7x, 32 devices: a whole 2x2x4 slice. The times are simulated.
32 devices in a mesh: row: 4 (over y, x), col: 8 (over z, core).
Axes of the slice: x: 2, y: 2, z: 4, core: 2. Of those that a mesh axis runs over, the one named last changes fastest.
Arguments:
- loads: float32 [4, 8, 1024, 8], P('row', 'col'), may hold values from -6 to 6
- schur: float32 [4, 8, 1024, 1024], P('row', 'col'), may hold values from -0.5 to 4.5, as said below
- factor: float32 [4, 8, 1024, 1024], P('row', 'col'), may hold values from -0.5 to 0.6, as said below
- coarse_inverse: float32 [1536, 1536], P(('row', 'col')), may hold values from -0.5 to 1.5, as said below
- elements: int32 [4, 8], P('row', 'col'), may hold values from 4096 to 16383
- west_map: int32 [4, 8, 256], P('row', 'col'), may hold values from 0 to 255, each once within a row
- south_map: int32 [4, 8, 256], P('row', 'col'), may hold values from 0 to 255, each once within a row
- prim_local: int32 [4, 8, 48], P('row', 'col'), may hold values from 0 to 1023
- prim_coarse: int32 [4, 8, 48], P('row', 'col'), may hold values from 0 to 1535
Outputs:
- solution: float32 [4, 8, 1024, 8], P('row', 'col')
- residual: float32 [4, 8, 1024, 8], P('row', 'col')
Inputs may be any that keep to these rules, and one draw needn't show every extreme that they name: `schur`: symmetric positive definite. `factor`: symmetric positive definite. `coarse_inverse`: symmetric positive definite. `west_map`: each subdomain's row is a permutation of 0 to 255. `south_map`: each subdomain's row is a permutation of 0 to 255. `prim_local`: values may repeat. `prim_coarse`: values may repeat, within a subdomain and between subdomains.
All inputs are finite; a program needn't handle non-finite values.
Results may differ from a plain program's by a relative error of at most 0.0001.
Values sent between devices are 32-bit elements; how exact they have to be, the bound alone decides.
A program may use at most 128 MiB of HBM per device.

v0:
```python
import jax
import jax.numpy as jnp
from jax import lax
from jax.sharding import PartitionSpec as P

ELEM_BASE = 4096
HIGHEST_PRECISION = lax.Precision.HIGHEST


def from_behind(x, axis, by):
    devices = lax.axis_size(axis)
    pairs = [(i, i + by) for i in range(devices) if 0 <= i + by < devices]
    return lax.ppermute(x, axis, pairs)


def product(matrix, vectors):
    return jnp.dot(matrix, vectors, precision=HIGHEST_PRECISION, preferred_element_type=jnp.float32)


def body(
    loads, schur, factor, coarse_inverse, elements, west_map, south_map, prim_local, prim_coarse
):
    schur_block = schur[0, 0]
    factor_block = factor[0, 0]
    local_loads = loads[0, 0]
    sweep_count = elements[0, 0] // ELEM_BASE
    west_order = west_map[0, 0]
    south_order = south_map[0, 0]
    primal_local = prim_local[0, 0]
    primal_coarse = prim_coarse[0, 0]
    unknowns = schur_block.shape[0]
    face_size = unknowns // 4
    column = lax.axis_index("col")
    grid_row = lax.axis_index("row")
    neighbour_flags = jnp.stack(
        [
            column > 0,
            column < lax.axis_size("col") - 1,
            grid_row > 0,
            grid_row < lax.axis_size("row") - 1,
        ]
    )
    weights = jnp.where(neighbour_flags[jnp.arange(unknowns) // face_size], 0.5, 1.0).astype(
        jnp.float32
    )[:, None]

    def assemble(values):
        west_face = values[:face_size]
        east_face = values[face_size : 2 * face_size]
        south_face = values[2 * face_size : 3 * face_size]
        north_face = values[3 * face_size :]
        from_west = from_behind(east_face, "col", 1)
        west_add = jnp.take(from_west, west_order, axis=0)
        west_back = jnp.zeros_like(west_face).at[west_order].set(west_face)
        from_east = from_behind(west_back, "col", -1)
        from_south = from_behind(north_face, "row", 1)
        south_add = jnp.take(from_south, south_order, axis=0)
        south_back = jnp.zeros_like(south_face).at[south_order].set(south_face)
        from_north = from_behind(south_back, "row", -1)
        return values + jnp.concatenate([west_add, from_east, south_add, from_north], axis=0)

    def weighted_sum(first, second):
        return jnp.sum(weights * first * second, axis=0)

    all_primal = lax.all_gather(primal_coarse, ("row", "col"), axis=0, tiled=True)
    right_side = assemble(local_loads)
    residual = right_side
    scaled = weights * residual
    local = product(factor_block, scaled)

    def sweep(turn, present):
        return present + product(factor_block, scaled - product(schur_block, present))

    local = lax.fori_loop(1, sweep_count, sweep, local)
    picked = jnp.take(scaled, primal_local, axis=0)
    columns = jnp.take(coarse_inverse, all_primal, axis=1)
    solved = product(columns, lax.all_gather(picked, ("row", "col"), axis=0, tiled=True))
    whole = lax.all_gather(solved, ("row", "col"), axis=0, tiled=True)
    precond = assemble(
        weights
        * (
            local
            + jnp.zeros_like(scaled).at[primal_local].add(jnp.take(whole, primal_coarse, axis=0))
        )
    )
    product_now = lax.psum(weighted_sum(residual, precond), ("row", "col"))
    image = assemble(product(schur_block, precond))
    alpha = product_now / lax.psum(weighted_sum(precond, image), ("row", "col"))
    solution = alpha * precond
    residual = residual - alpha * image
    return (solution[None, None], residual[None, None])


def solution(mesh):
    placed = (
        P("row", "col", None, None),
        P("row", "col", None, None),
        P("row", "col", None, None),
        P(("row", "col"), None),
        P("row", "col"),
        P("row", "col", None),
        P("row", "col", None),
        P("row", "col", None),
        P("row", "col", None),
    )
    return jax.shard_map(
        body,
        mesh=mesh,
        in_specs=placed,
        out_specs=(P("row", "col", None, None), P("row", "col", None, None)),
        check_vma=False,
    )
```

profile of v0, /device:TPU:0, one launch (start us, length us, event | category | flops | bytes accessed | tf_op | source)
XLA Modules:
  0.0 256.3 jit_solution(8718719181798448319)
XLA Ops:
  3.5 1.3 collective-permute-start.1
  6.8 1.3 collective-permute-start.3
  8.3 5.5 %collective-permute-start.2 = (f32[256,8]{1,0:T(8,128)S(1)}, f32[256,8]{1,0:T(8,128)S(1)}, u32[]{:S(2)}, u32[]{:S(2)}) collective-permute-start(f32[256,8]{1,0:T(8,128)S(1)} %bitcast.105), channel_id=1, source_target_pairs={{0,8},{8,16},{16,24},{1,9},{9,17},{17,25},{2,10},{10,18},{18,26},{... | collective-permute-start | bytes 24584 | tf_op jit(solution)/shard_map/ppermute | solution.py:13
  13.9 2.8 %collective-permute-start = (f32[256,8]{1,0:T(8,128)S(1)}, f32[256,8]{1,0:T(8,128)S(1)}, u32[]{:S(2)}, u32[]{:S(2)}) collective-permute-start(f32[256,8]{1,0:T(8,128)S(1)} %bitcast.104), channel_id=1, source_target_pairs={{0,1},{1,2},{2,3},{3,4},{4,5},{5,6},{6,7},{8,9},{9,10},{10,11},{11... | collective-permute-start | bytes 24584 | tf_op jit(solution)/shard_map/ppermute | solution.py:13
  22.8 41.8 %all-reduce = s32[1536]{0:T(1024)S(1)} all-reduce(s32[1536]{0:T(1024)S(1)} %bitcast_dynamic-update-slice_fusion), channel_id=2, replica_groups=mesh['row'=4,'col'=8] {'row','col'}, use_global_device_ids=true, to_apply=%add | all-reduce | flops 1536 | bytes 12288 | tf_op jit(solution)/shard_map/all_gather | solution.py:65
  66.6 2.6 %gather_fusion = f32[1536,48]{1,0:T(8,128)S(1)} fusion(f32[48,1536]{0,1:T(8,128)S(1)} %copy.96, s32[2048]{0:T(1024)S(1)} %pad_clamp_fusion), kind=kCustom, calls=%fused_computation.6 | custom fusion | bytes 595968 | tf_op jit(solution)/shard_map/jit(_take)/gather | solution.py:76
  71.1 5.7 %convolution_bitcast_fusion.2 = f32[1024,8]{0,1:T(8,128)S(1)} fusion(f32[1,1,1024,8]{2,3,1,0:T(8,128)S(1)} %copy-done.1, f32[1,1,256,8]{2,3,1,0:T(8,128)S(1)} %bitcast.107, f32[1,1,256,8]{2,3,1,0:T(8,128)S(1)} %bitcast.102, f32[1,1,256,8]{2,3,1,0:T(8,128)S(1)} %bitcast.106, f32[1,1,256,8]{2,3,1,0:T(8,128)S(1)} %bitcast.103, f32[1024]{0:T(1024)S(1)} %bitcast.98, ...), kind=kOutput, calls=%fused_computation.20 | convolution fusion | flops 100704256 | bytes 4296704 | tf_op jit(solution)/shard_map/dot_general | solution.py:17
  76.8 19.1 %while.10 = (s32[]{:T(128)}, f32[1024,8]{0,1:T(8,128)S(1)}, s32[]{:T(128)}, f32[1024,1024]{1,0:T(8,128)}, f32[1024,8]{0,1:T(8,128)S(1)}, /*index=5*/f32[1024,1024]{1,0:T(8,128)}, s32[]{:T(128)}) while((s32[]{:T(128)}, f32[1024,8]{0,1:T(8,128)S(1)}, s32[]{:T(128)}, f32[1024,1024]{1,0:T(8,128)}, f32[1024,8]{0,1:T(8,128)S(1)}, ...), condition=%wide.region_3.5_spmd, body=%wide.region_2.4_spmd.sunk | while | flops 201342976 | bytes 25362536 | solution.py:74
  76.9 5.9 %convolution_subtract_fusion.2 = f32[1024,8]{0,1:T(8,128)S(1)} fusion(f32[1024,8]{0,1:T(8,128)S(1)} %get-tuple-element.125, f32[1024,1024]{1,0:T(8,128)} %get-tuple-element.124, f32[1024,8]{0,1:T(8,128)S(1)} %get-tuple-element.115), kind=kOutput, calls=%fused_computation.18.clone.1 | convolution fusion | flops 100671488 | bytes 4292608 | tf_op jit(solution)/shard_map/while/body/dot_general | solution.py:17
  82.8 3.6 %fusion.55 = f32[1024,8]{0,1:T(8,128)S(1)} fusion(f32[1024,8]{0,1:T(8,128)S(1)} %get-tuple-element.115, f32[1024,8]{0,1:T(8,128)S(1)} %convolution_subtract_fusion.2, f32[1024,1024]{1,0:T(8,128)S(1)} %copy-done), kind=kOutput, calls=%fused_computation.17.clone.1 | convolution fusion | flops 100671488 | bytes 4292608 | tf_op jit(solution)/shard_map/while/body/dot_general | solution.py:17
  86.4 5.9 %convolution_subtract_fusion.2 = f32[1024,8]{0,1:T(8,128)S(1)} fusion(f32[1024,8]{0,1:T(8,128)S(1)} %get-tuple-element.125, f32[1024,1024]{1,0:T(8,128)} %get-tuple-element.124, f32[1024,8]{0,1:T(8,128)S(1)} %get-tuple-element.115), kind=kOutput, calls=%fused_computation.18.clone.1 | convolution fusion | flops 100671488 | bytes 4292608 | tf_op jit(solution)/shard_map/while/body/dot_general | solution.py:17
  92.3 3.6 %fusion.55 = f32[1024,8]{0,1:T(8,128)S(1)} fusion(f32[1024,8]{0,1:T(8,128)S(1)} %get-tuple-element.115, f32[1024,8]{0,1:T(8,128)S(1)} %convolution_subtract_fusion.2, f32[1024,1024]{1,0:T(8,128)S(1)} %copy-done), kind=kOutput, calls=%fused_computation.17.clone.1 | convolution fusion | flops 100671488 | bytes 4292608 | tf_op jit(solution)/shard_map/while/body/dot_general | solution.py:17
  96.8 37.1 %all-gather.1 = f32[32,48,8]{1,2,0:T(8,128)S(1)} all-gather(f32[1,48,8]{1,2,0:T(8,128)S(1)} %copy.98), channel_id=1, replica_groups=mesh['row'=4,'col'=8] {'row','col'}, dimensions={0}, use_global_device_ids=true | all-gather | bytes 50688 | tf_op jit(solution)/shard_map/all_gather | solution.py:77
  134.7 38.6 %all-gather.2 = f32[32,48,8]{1,2,0:T(8,128)S(1)} all-gather(f32[1,48,8]{1,2,0:T(8,128)S(1)} %convolution_bitcast_fusion.3), channel_id=1, replica_groups=mesh['row'=4,'col'=8] {'row','col'}, dimensions={0}, use_global_device_ids=true | all-gather | bytes 50688 | tf_op jit(solution)/shard_map/all_gather | solution.py:78
  176.1 2.2 collective-permute-start.4
  179.8 1.3 collective-permute-start.7
  182.5 1.5 collective-permute-start.5
  185.9 3.0 %collective-permute-done.7 = f32[256,8]{0,1:T(8,128)S(1)} collective-permute-done((f32[256,8]{0,1:T(8,128)S(1)}, f32[256,8]{0,1:T(8,128)S(1)}, u32[]{:S(2)}, u32[]{:S(2)}) %collective-permute-start.7) | collective-permute-done | bytes 8224 | tf_op jit(solution)/shard_map/ppermute | solution.py:13
  188.9 5.6 %convolution_bitcast_fusion.1 = f32[1024,8]{0,1:T(8,128)S(1)} fusion(f32[1024,8]{0,1:T(8,128)S(1)} %maximum_add_fusion.2, f32[1,1,1024,1024]{3,2,1,0:T(8,128)} %bitcast.95), kind=kOutput, calls=%fused_computation.19 | convolution fusion | flops 100663296 | bytes 4259840 | tf_op jit(solution)/shard_map/dot_general | solution.py:17
  194.6 5.9 %collective-permute-start.10 = (f32[256,8]{0,1:T(8,128)S(1)}, f32[256,8]{0,1:T(8,128)S(1)}, u32[]{:S(2)}, u32[]{:S(2)}) collective-permute-start(f32[256,8]{0,1:T(8,128)S(1)} %get-tuple-element.55), channel_id=1, source_target_pairs={{0,8},{8,16},{16,24},{1,9},{9,17},{17,25},{2,10},{10,18},{18,26},{... | collective-permute-start | bytes 24584 | tf_op jit(solution)/shard_map/ppermute | solution.py:13
  200.6 4.0 %collective-permute-start.8 = (f32[256,8]{0,1:T(8,128)S(1)}, f32[256,8]{0,1:T(8,128)S(1)}, u32[]{:S(2)}, u32[]{:S(2)}) collective-permute-start(f32[256,8]{0,1:T(8,128)S(1)} %get-tuple-element.53), channel_id=1, source_target_pairs={{0,1},{1,2},{2,3},{3,4},{4,5},{5,6},{6,7},{8,9},{9,10},{10,11},{11... | collective-permute-start | bytes 24584 | tf_op jit(solution)/shard_map/ppermute | solution.py:13
  206.0 1.3 collective-permute-start.11
  208.7 1.3 collective-permute-start.9
  212.5 43.1 %all-reduce.1 = (f32[8]{0:T(128)S(1)}, f32[8]{0:T(128)S(1)}) all-reduce(f32[8]{0:T(128)S(1)} %get-tuple-element.38, f32[8]{0:T(128)S(1)} %get-tuple-element.37), channel_id=1, replica_groups=mesh['row'=4,'col'=8] {'row','col'}, use_global_device_ids=true, to_apply=%region_8.10 | all-reduce | flops 16 | bytes 128 | tf_op jit(solution)/shard_map/psum | solution.py:86
  (100 shorter events, 29.5 us)
Async XLA Ops:
  0.6 70.3 %copy-start.1 = (f32[1,1,1024,8]{2,3,1,0:T(8,128)S(1)}, f32[1,1,1024,8]{2,3,1,0:T(8,128)}, u32[]{:S(2)}) copy-start(f32[1,1,1024,8]{2,3,1,0:T(8,128)} %param.13) | copy-start | bytes 98308
  3.5 67.4 %collective-permute-start.1 = (f32[256,8]{0,1:T(8,128)S(1)}, f32[256,8]{0,1:T(8,128)S(1)}, u32[]{:S(2)}, u32[]{:S(2)}) collective-permute-start(f32[256,8]{0,1:T(8,128)S(1)} %copy.91), channel_id=1, source_target_pairs={{1,0},{2,1},{3,2},{4,3},{5,4},{6,5},{7,6},{9,8},{10,9},{11,10},{12... | collective-permute-start | bytes 24584 | tf_op jit(solution)/shard_map/ppermute | solution.py:13
  6.8 64.0 %collective-permute-start.3 = (f32[256,8]{0,1:T(8,128)S(1)}, f32[256,8]{0,1:T(8,128)S(1)}, u32[]{:S(2)}, u32[]{:S(2)}) collective-permute-start(f32[256,8]{0,1:T(8,128)S(1)} %copy.95), channel_id=1, source_target_pairs={{8,0},{16,8},{24,16},{9,1},{17,9},{25,17},{10,2},{18,10},{26,18},{... | collective-permute-start | bytes 24584 | tf_op jit(solution)/shard_map/ppermute | solution.py:13
  8.3 61.0 %collective-permute-start.2 = (f32[256,8]{1,0:T(8,128)S(1)}, f32[256,8]{1,0:T(8,128)S(1)}, u32[]{:S(2)}, u32[]{:S(2)}) collective-permute-start(f32[256,8]{1,0:T(8,128)S(1)} %bitcast.105), channel_id=1, source_target_pairs={{0,8},{8,16},{16,24},{1,9},{9,17},{17,25},{2,10},{10,18},{18,26},{... | collective-permute-start | bytes 24584 | tf_op jit(solution)/shard_map/ppermute | solution.py:13
  13.9 56.1 %collective-permute-start = (f32[256,8]{1,0:T(8,128)S(1)}, f32[256,8]{1,0:T(8,128)S(1)}, u32[]{:S(2)}, u32[]{:S(2)}) collective-permute-start(f32[256,8]{1,0:T(8,128)S(1)} %bitcast.104), channel_id=1, source_target_pairs={{0,1},{1,2},{2,3},{3,4},{4,5},{5,6},{6,7},{8,9},{9,10},{10,11},{11... | collective-permute-start | bytes 24584 | tf_op jit(solution)/shard_map/ppermute | solution.py:13
  76.9 5.9 %copy-start = (f32[1024,1024]{1,0:T(8,128)S(1)}, f32[1024,1024]{1,0:T(8,128)}, u32[]{:S(2)}) copy-start(f32[1024,1024]{1,0:T(8,128)} %get-tuple-element.126) | copy-start | bytes 12582916 | tf_op jit(solution)/shard_map/while
  86.4 5.9 %copy-start = (f32[1024,1024]{1,0:T(8,128)S(1)}, f32[1024,1024]{1,0:T(8,128)}, u32[]{:S(2)}) copy-start(f32[1024,1024]{1,0:T(8,128)} %get-tuple-element.126) | copy-start | bytes 12582916 | tf_op jit(solution)/shard_map/while
  174.9 9.1 %collective-permute-start.6 = (f32[256,8]{0,1:T(8,128)S(1)}, f32[256,8]{0,1:T(8,128)S(1)}, u32[]{:S(2)}, u32[]{:S(2)}) collective-permute-start(f32[256,8]{0,1:T(8,128)S(1)} %get-tuple-element.59), channel_id=1, source_target_pairs={{0,8},{8,16},{16,24},{1,9},{9,17},{17,25},{2,10},{10,18},{18,26},{... | collective-permute-start | bytes 24584 | tf_op jit(solution)/shard_map/ppermute | solution.py:13
  176.1 8.8 %collective-permute-start.4 = (f32[256,8]{0,1:T(8,128)S(1)}, f32[256,8]{0,1:T(8,128)S(1)}, u32[]{:S(2)}, u32[]{:S(2)}) collective-permute-start(f32[256,8]{0,1:T(8,128)S(1)} %get-tuple-element.57), channel_id=1, source_target_pairs={{0,1},{1,2},{2,3},{3,4},{4,5},{5,6},{6,7},{8,9},{9,10},{10,11},{11... | collective-permute-start | bytes 24584 | tf_op jit(solution)/shard_map/ppermute | solution.py:13
  179.8 9.1 %collective-permute-start.7 = (f32[256,8]{0,1:T(8,128)S(1)}, f32[256,8]{0,1:T(8,128)S(1)}, u32[]{:S(2)}, u32[]{:S(2)}) collective-permute-start(f32[256,8]{0,1:T(8,128)S(1)} %copy.111), channel_id=1, source_target_pairs={{8,0},{16,8},{24,16},{9,1},{17,9},{25,17},{10,2},{18,10},{26,18},{... | collective-permute-start | bytes 24584 | tf_op jit(solution)/shard_map/ppermute | solution.py:13
  182.5 6.4 %collective-permute-start.5 = (f32[256,8]{0,1:T(8,128)S(1)}, f32[256,8]{0,1:T(8,128)S(1)}, u32[]{:S(2)}, u32[]{:S(2)}) collective-permute-start(f32[256,8]{0,1:T(8,128)S(1)} %copy.107), channel_id=1, source_target_pairs={{1,0},{2,1},{3,2},{4,3},{5,4},{6,5},{7,6},{9,8},{10,9},{11,10},{12... | collective-permute-start | bytes 24584 | tf_op jit(solution)/shard_map/ppermute | solution.py:13
  194.6 15.4 %collective-permute-start.10 = (f32[256,8]{0,1:T(8,128)S(1)}, f32[256,8]{0,1:T(8,128)S(1)}, u32[]{:S(2)}, u32[]{:S(2)}) collective-permute-start(f32[256,8]{0,1:T(8,128)S(1)} %get-tuple-element.55), channel_id=1, source_target_pairs={{0,8},{8,16},{16,24},{1,9},{9,17},{17,25},{2,10},{10,18},{18,26},{... | collective-permute-start | bytes 24584 | tf_op jit(solution)/shard_map/ppermute | solution.py:13
  200.6 10.4 %collective-permute-start.8 = (f32[256,8]{0,1:T(8,128)S(1)}, f32[256,8]{0,1:T(8,128)S(1)}, u32[]{:S(2)}, u32[]{:S(2)}) collective-permute-start(f32[256,8]{0,1:T(8,128)S(1)} %get-tuple-element.53), channel_id=1, source_target_pairs={{0,1},{1,2},{2,3},{3,4},{4,5},{5,6},{6,7},{8,9},{9,10},{10,11},{11... | collective-permute-start | bytes 24584 | tf_op jit(solution)/shard_map/ppermute | solution.py:13
  206.0 6.2 %collective-permute-start.11 = (f32[256,8]{0,1:T(8,128)S(1)}, f32[256,8]{0,1:T(8,128)S(1)}, u32[]{:S(2)}, u32[]{:S(2)}) collective-permute-start(f32[256,8]{0,1:T(8,128)S(1)} %copy.119), channel_id=1, source_target_pairs={{8,0},{16,8},{24,16},{9,1},{17,9},{25,17},{10,2},{18,10},{26,18},{... | collective-permute-start | bytes 24584 | tf_op jit(solution)/shard_map/ppermute | solution.py:13
  208.7 3.7 %collective-permute-start.9 = (f32[256,8]{0,1:T(8,128)S(1)}, f32[256,8]{0,1:T(8,128)S(1)}, u32[]{:S(2)}, u32[]{:S(2)}) collective-permute-start(f32[256,8]{0,1:T(8,128)S(1)} %copy.115), channel_id=1, source_target_pairs={{1,0},{2,1},{3,2},{4,3},{5,4},{6,5},{7,6},{9,8},{10,9},{11,10},{12... | collective-permute-start | bytes 24584 | tf_op jit(solution)/shard_map/ppermute | solution.py:13
where the time goes:
time: 257 us; the launch traced here: 256 us
  blocking collectives  161 us (63%)
  matrix products  30.9 us (12%)
  starting transfers between devices  29.8 us (12%)
  local copies, waits for them, and re-layouts  20.7 us (8%)
  other arithmetic  8.95 us (3%)
  waiting for transfers between devices  3.55 us (1%)
    psum x1, blocking collectives, body(): product_now = lax.psum(weighted_sum(residual, precond), ('row', 'col'))  43.1 us
    all_gather x1, blocking collectives, body(): lax.all_gather(primal_coarse, ('row', 'col'), axis=0, tiled=True)  41.8 us
    all_gather x1, blocking collectives, body(): whole = lax.all_gather(solved, ('row', 'col'), axis=0, tiled=True)  38.6 us
    all_gather x1, blocking collectives, body(): lax.all_gather(picked, ('row', 'col'), axis=0, tiled=True)  37.1 us
    dot_general x7, matrix products, product(): jnp.dot(matrix, vectors, precision=HIGHEST_PRECISION, preferred_element_t...  30.9 us
    ppermute x12, starting transfers between devices, from_behind(): return lax.ppermute(x, axis, pairs)  29.8 us
  transfers between devices with their start and end apart: 12, of which 3 were waited for; matrix products, arithmetic and copies ran while one was open for 9% of the time, Pallas kernels for 0%

commit v1 on v0

--- a/solution.py
+++ b/solution.py
@@ -83,7 +83,7 @@
             + jnp.zeros_like(scaled).at[primal_local].add(jnp.take(whole, primal_coarse, axis=0))
         )
     )
-    product_now = lax.psum(weighted_sum(residual, precond), ("row", "col"))
+    product_now = lax.psum(lax.psum(weighted_sum(residual, precond), "row"), "col")
     image = assemble(product(schur_block, precond))
     alpha = product_now / lax.psum(weighted_sum(precond, image), ("row", "col"))
     solution = alpha * precond

time: 257 us -> 280 us (1.089)
  blocking collectives: 161 us -> 184 us
    psum x1 -> x3, blocking collectives: 43.1 us -> 66.2 us  [the longest x1 41.7 us: body(): alpha = product_now / lax.psum(weighted_sum(precond, image), ('row', 'col'))]
  transfers between devices with their start and end apart: 12 -> 12, of which waited for: 3 -> 3; matrix products, arithmetic and copies ran while one was open for 9% -> 8% of each run, Pallas kernels for 0% -> 0%
where the time goes in v1:
time: 280 us; the launch traced here: 279 us
  blocking collectives  184 us (66%)
  matrix products  30.9 us (11%)
  starting transfers between devices  29.8 us (11%)
  local copies, waits for them, and re-layouts  20.7 us (7%)
  other arithmetic  8.95 us (3%)
  waiting for transfers between devices  3.55 us (1%)
    all_gather x1, blocking collectives, body(): lax.all_gather(primal_coarse, ('row', 'col'), axis=0, tiled=True)  41.8 us
    psum x1, blocking collectives, body(): alpha = product_now / lax.psum(weighted_sum(precond, image), ('row', 'col'))  41.7 us
    all_gather x1, blocking collectives, body(): whole = lax.all_gather(solved, ('row', 'col'), axis=0, tiled=True)  38.6 us
    all_gather x1, blocking collectives, body(): lax.all_gather(picked, ('row', 'col'), axis=0, tiled=True)  37.1 us
    dot_general x7, matrix products, product(): jnp.dot(matrix, vectors, precision=HIGHEST_PRECISION, preferred_element_t...  30.9 us
    ppermute x12, starting transfers between devices, from_behind(): return lax.ppermute(x, axis, pairs)  29.8 us
    psum x1, blocking collectives, body(): lax.psum(lax.psum(weighted_sum(residual, precond), 'row'), 'col')  13.7 us
    psum x1, blocking collectives, body(): lax.psum(weighted_sum(residual, precond), 'row')  10.7 us
  transfers between devices with their start and end apart: 12, of which 3 were waited for; matrix products, arithmetic and copies ran while one was open for 8% of the time, Pallas kernels for 0%

profile of v1, /device:TPU:0, one launch (start us, length us, event | category | flops | bytes accessed | tf_op | source)
XLA Modules:
  0.0 279.4 jit_solution(9304066787464615929)
XLA Ops:
  3.5 1.3 collective-permute-start.1
  6.8 1.3 collective-permute-start.3
  8.3 5.5 %collective-permute-start.2 = (f32[256,8]{1,0:T(8,128)S(1)}, f32[256,8]{1,0:T(8,128)S(1)}, u32[]{:S(2)}, u32[]{:S(2)}) collective-permute-start(f32[256,8]{1,0:T(8,128)S(1)} %bitcast.105), channel_id=1, source_target_pairs={{0,8},{8,16},{16,24},{1,9},{9,17},{17,25},{2,10},{10,18},{18,26},{... | collective-permute-start | bytes 24584 | tf_op jit(solution)/shard_map/ppermute | solution.py:13
  13.9 2.8 collective-permute-start
  22.8 41.8 %all-reduce = s32[1536]{0:T(1024)S(1)} all-reduce(s32[1536]{0:T(1024)S(1)} %bitcast_dynamic-update-slice_fusion), channel_id=2, replica_groups=mesh['row'=4,'col'=8] {'row','col'}, use_global_device_ids=true, to_apply=%add | all-reduce | flops 1536 | bytes 12288 | tf_op jit(solution)/shard_map/all_gather | solution.py:65
  66.6 2.6 gather_fusion
  71.1 5.7 %convolution_bitcast_fusion.2 = f32[1024,8]{0,1:T(8,128)S(1)} fusion(f32[1,1,1024,8]{2,3,1,0:T(8,128)S(1)} %copy-done.1, f32[1,1,256,8]{2,3,1,0:T(8,128)S(1)} %bitcast.107, f32[1,1,256,8]{2,3,1,0:T(8,128)S(1)} %bitcast.102, f32[1,1,256,8]{2,3,1,0:T(8,128)S(1)} %bitcast.106, f32[1,1,256,8]{2,3,1,0:T(8,128)S(1)} %bitcast.103, f32[1024]{0:T(1024)S(1)} %bitcast.98, ...), kind=kOutput, calls=%fused_computation.20 | convolution fusion | flops 100704256 | bytes 4296704 | tf_op jit(solution)/shard_map/dot_general | solution.py:17
  76.8 19.1 %while.10 = (s32[]{:T(128)}, f32[1024,8]{0,1:T(8,128)S(1)}, s32[]{:T(128)}, f32[1024,1024]{1,0:T(8,128)}, f32[1024,8]{0,1:T(8,128)S(1)}, /*index=5*/f32[1024,1024]{1,0:T(8,128)}, s32[]{:T(128)}) while((s32[]{:T(128)}, f32[1024,8]{0,1:T(8,128)S(1)}, s32[]{:T(128)}, f32[1024,1024]{1,0:T(8,128)}, f32[1024,8]{0,1:T(8,128)S(1)}, ...), condition=%wide.region_3.5_spmd, body=%wide.region_2.4_spmd.sunk | while | flops 201342976 | bytes 25362536 | solution.py:74
  76.9 5.9 %convolution_subtract_fusion.2 = f32[1024,8]{0,1:T(8,128)S(1)} fusion(f32[1024,8]{0,1:T(8,128)S(1)} %get-tuple-element.123, f32[1024,1024]{1,0:T(8,128)} %get-tuple-element.122, f32[1024,8]{0,1:T(8,128)S(1)} %get-tuple-element.113), kind=kOutput, calls=%fused_computation.18.clone.1 | convolution fusion | flops 100671488 | bytes 4292608 | tf_op jit(solution)/shard_map/while/body/dot_general | solution.py:17
  82.8 3.6 %fusion.55 = f32[1024,8]{0,1:T(8,128)S(1)} fusion(f32[1024,8]{0,1:T(8,128)S(1)} %get-tuple-element.113, f32[1024,8]{0,1:T(8,128)S(1)} %convolution_subtract_fusion.2, f32[1024,1024]{1,0:T(8,128)S(1)} %copy-done), kind=kOutput, calls=%fused_computation.17.clone.1 | convolution fusion | flops 100671488 | bytes 4292608 | tf_op jit(solution)/shard_map/while/body/dot_general | solution.py:17
  86.4 5.9 %convolution_subtract_fusion.2 = f32[1024,8]{0,1:T(8,128)S(1)} fusion(f32[1024,8]{0,1:T(8,128)S(1)} %get-tuple-element.123, f32[1024,1024]{1,0:T(8,128)} %get-tuple-element.122, f32[1024,8]{0,1:T(8,128)S(1)} %get-tuple-element.113), kind=kOutput, calls=%fused_computation.18.clone.1 | convolution fusion | flops 100671488 | bytes 4292608 | tf_op jit(solution)/shard_map/while/body/dot_general | solution.py:17
  92.3 3.6 %fusion.55 = f32[1024,8]{0,1:T(8,128)S(1)} fusion(f32[1024,8]{0,1:T(8,128)S(1)} %get-tuple-element.113, f32[1024,8]{0,1:T(8,128)S(1)} %convolution_subtract_fusion.2, f32[1024,1024]{1,0:T(8,128)S(1)} %copy-done), kind=kOutput, calls=%fused_computation.17.clone.1 | convolution fusion | flops 100671488 | bytes 4292608 | tf_op jit(solution)/shard_map/while/body/dot_general | solution.py:17
  96.8 37.1 %all-gather.1 = f32[32,48,8]{1,2,0:T(8,128)S(1)} all-gather(f32[1,48,8]{1,2,0:T(8,128)S(1)} %copy.98), channel_id=1, replica_groups=mesh['row'=4,'col'=8] {'row','col'}, dimensions={0}, use_global_device_ids=true | all-gather | bytes 50688 | tf_op jit(solution)/shard_map/all_gather | solution.py:77
  134.7 38.6 %all-gather.2 = f32[32,48,8]{1,2,0:T(8,128)S(1)} all-gather(f32[1,48,8]{1,2,0:T(8,128)S(1)} %convolution_bitcast_fusion.3), channel_id=1, replica_groups=mesh['row'=4,'col'=8] {'row','col'}, dimensions={0}, use_global_device_ids=true | all-gather | bytes 50688 | tf_op jit(solution)/shard_map/all_gather | solution.py:78
  176.1 2.2 collective-permute-start.4
  179.8 1.3 collective-permute-start.7
  182.5 1.5 collective-permute-start.5
  185.9 3.0 %collective-permute-done.7 = f32[256,8]{0,1:T(8,128)S(1)} collective-permute-done((f32[256,8]{0,1:T(8,128)S(1)}, f32[256,8]{0,1:T(8,128)S(1)}, u32[]{:S(2)}, u32[]{:S(2)}) %collective-permute-start.7) | collective-permute-done | bytes 8224 | tf_op jit(solution)/shard_map/ppermute | solution.py:13
  188.9 5.6 %convolution_bitcast_fusion.1 = f32[1024,8]{0,1:T(8,128)S(1)} fusion(f32[1024,8]{0,1:T(8,128)S(1)} %maximum_add_fusion.2, f32[1,1,1024,1024]{3,2,1,0:T(8,128)} %bitcast.95), kind=kOutput, calls=%fused_computation.19 | convolution fusion | flops 100663296 | bytes 4259840 | tf_op jit(solution)/shard_map/dot_general | solution.py:17
  194.6 5.9 %collective-permute-start.10 = (f32[256,8]{0,1:T(8,128)S(1)}, f32[256,8]{0,1:T(8,128)S(1)}, u32[]{:S(2)}, u32[]{:S(2)}) collective-permute-start(f32[256,8]{0,1:T(8,128)S(1)} %get-tuple-element.53), channel_id=1, source_target_pairs={{0,8},{8,16},{16,24},{1,9},{9,17},{17,25},{2,10},{10,18},{18,26},{... | collective-permute-start | bytes 24584 | tf_op jit(solution)/shard_map/ppermute | solution.py:13
  200.6 4.0 %collective-permute-start.8 = (f32[256,8]{0,1:T(8,128)S(1)}, f32[256,8]{0,1:T(8,128)S(1)}, u32[]{:S(2)}, u32[]{:S(2)}) collective-permute-start(f32[256,8]{0,1:T(8,128)S(1)} %get-tuple-element.51), channel_id=1, source_target_pairs={{0,1},{1,2},{2,3},{3,4},{4,5},{5,6},{6,7},{8,9},{9,10},{10,11},{11... | collective-permute-start | bytes 24584 | tf_op jit(solution)/shard_map/ppermute | solution.py:13
  212.5 10.7 %psum.21 = f32[8]{0:T(128)S(1)} all-reduce(f32[8]{0:T(128)S(1)} %get-tuple-element.38), channel_id=1, replica_groups=mesh['row'=4,'col'=8] {'row'}, use_global_device_ids=true, to_apply=%region_8.10 | all-reduce | flops 8 | bytes 64 | tf_op jit(solution)/shard_map/psum | solution.py:86
  223.2 41.7 %psum.23 = f32[8]{0:T(128)S(1)} all-reduce(f32[8]{0:T(128)S(1)} %get-tuple-element.37), channel_id=1, replica_groups=mesh['row'=4,'col'=8] {'row','col'}, use_global_device_ids=true, to_apply=%region_13.15 | all-reduce | flops 8 | bytes 64 | tf_op jit(solution)/shard_map/psum | solution.py:88
  264.9 13.7 %psum.22 = f32[8]{0:T(128)S(1)} all-reduce(f32[8]{0:T(128)S(1)} %psum.21), channel_id=1, replica_groups=mesh['row'=4,'col'=8] {'col'}, use_global_device_ids=true, to_apply=%region_9.11 | all-reduce | flops 8 | bytes 64 | tf_op jit(solution)/shard_map/psum | solution.py:86
  (102 shorter events, 32.1 us)
Async XLA Ops:
  0.6 70.3 %copy-start.1 = (f32[1,1,1024,8]{2,3,1,0:T(8,128)S(1)}, f32[1,1,1024,8]{2,3,1,0:T(8,128)}, u32[]{:S(2)}) copy-start(f32[1,1,1024,8]{2,3,1,0:T(8,128)} %param.13) | copy-start | bytes 98308
  3.5 67.4 %collective-permute-start.1 = (f32[256,8]{0,1:T(8,128)S(1)}, f32[256,8]{0,1:T(8,128)S(1)}, u32[]{:S(2)}, u32[]{:S(2)}) collective-permute-start(f32[256,8]{0,1:T(8,128)S(1)} %copy.91), channel_id=1, source_target_pairs={{1,0},{2,1},{3,2},{4,3},{5,4},{6,5},{7,6},{9,8},{10,9},{11,10},{12... | collective-permute-start | bytes 24584 | tf_op jit(solution)/shard_map/ppermute | solution.py:13
  6.8 64.0 %collective-permute-start.3 = (f32[256,8]{0,1:T(8,128)S(1)}, f32[256,8]{0,1:T(8,128)S(1)}, u32[]{:S(2)}, u32[]{:S(2)}) collective-permute-start(f32[256,8]{0,1:T(8,128)S(1)} %copy.95), channel_id=1, source_target_pairs={{8,0},{16,8},{24,16},{9,1},{17,9},{25,17},{10,2},{18,10},{26,18},{... | collective-permute-start | bytes 24584 | tf_op jit(solution)/shard_map/ppermute | solution.py:13
  8.3 61.0 %collective-permute-start.2 = (f32[256,8]{1,0:T(8,128)S(1)}, f32[256,8]{1,0:T(8,128)S(1)}, u32[]{:S(2)}, u32[]{:S(2)}) collective-permute-start(f32[256,8]{1,0:T(8,128)S(1)} %bitcast.105), channel_id=1, source_target_pairs={{0,8},{8,16},{16,24},{1,9},{9,17},{17,25},{2,10},{10,18},{18,26},{... | collective-permute-start | bytes 24584 | tf_op jit(solution)/shard_map/ppermute | solution.py:13
  13.9 56.1 %collective-permute-start = (f32[256,8]{1,0:T(8,128)S(1)}, f32[256,8]{1,0:T(8,128)S(1)}, u32[]{:S(2)}, u32[]{:S(2)}) collective-permute-start(f32[256,8]{1,0:T(8,128)S(1)} %bitcast.104), channel_id=1, source_target_pairs={{0,1},{1,2},{2,3},{3,4},{4,5},{5,6},{6,7},{8,9},{9,10},{10,11},{11... | collective-permute-start | bytes 24584 | tf_op jit(solution)/shard_map/ppermute | solution.py:13
  76.9 5.9 %copy-start = (f32[1024,1024]{1,0:T(8,128)S(1)}, f32[1024,1024]{1,0:T(8,128)}, u32[]{:S(2)}) copy-start(f32[1024,1024]{1,0:T(8,128)} %get-tuple-element.124) | copy-start | bytes 12582916 | tf_op jit(solution)/shard_map/while
  86.4 5.9 %copy-start = (f32[1024,1024]{1,0:T(8,128)S(1)}, f32[1024,1024]{1,0:T(8,128)}, u32[]{:S(2)}) copy-start(f32[1024,1024]{1,0:T(8,128)} %get-tuple-element.124) | copy-start | bytes 12582916 | tf_op jit(solution)/shard_map/while
  174.9 9.1 %collective-permute-start.6 = (f32[256,8]{0,1:T(8,128)S(1)}, f32[256,8]{0,1:T(8,128)S(1)}, u32[]{:S(2)}, u32[]{:S(2)}) collective-permute-start(f32[256,8]{0,1:T(8,128)S(1)} %get-tuple-element.57), channel_id=1, source_target_pairs={{0,8},{8,16},{16,24},{1,9},{9,17},{17,25},{2,10},{10,18},{18,26},{... | collective-permute-start | bytes 24584 | tf_op jit(solution)/shard_map/ppermute | solution.py:13
  176.1 8.8 %collective-permute-start.4 = (f32[256,8]{0,1:T(8,128)S(1)}, f32[256,8]{0,1:T(8,128)S(1)}, u32[]{:S(2)}, u32[]{:S(2)}) collective-permute-start(f32[256,8]{0,1:T(8,128)S(1)} %get-tuple-element.55), channel_id=1, source_target_pairs={{0,1},{1,2},{2,3},{3,4},{4,5},{5,6},{6,7},{8,9},{9,10},{10,11},{11... | collective-permute-start | bytes 24584 | tf_op jit(solution)/shard_map/ppermute | solution.py:13
  179.8 9.1 %collective-permute-start.7 = (f32[256,8]{0,1:T(8,128)S(1)}, f32[256,8]{0,1:T(8,128)S(1)}, u32[]{:S(2)}, u32[]{:S(2)}) collective-permute-start(f32[256,8]{0,1:T(8,128)S(1)} %copy.111), channel_id=1, source_target_pairs={{8,0},{16,8},{24,16},{9,1},{17,9},{25,17},{10,2},{18,10},{26,18},{... | collective-permute-start | bytes 24584 | tf_op jit(solution)/shard_map/ppermute | solution.py:13
  182.5 6.4 %collective-permute-start.5 = (f32[256,8]{0,1:T(8,128)S(1)}, f32[256,8]{0,1:T(8,128)S(1)}, u32[]{:S(2)}, u32[]{:S(2)}) collective-permute-start(f32[256,8]{0,1:T(8,128)S(1)} %copy.107), channel_id=1, source_target_pairs={{1,0},{2,1},{3,2},{4,3},{5,4},{6,5},{7,6},{9,8},{10,9},{11,10},{12... | collective-permute-start | bytes 24584 | tf_op jit(solution)/shard_map/ppermute | solution.py:13
  194.6 15.4 %collective-permute-start.10 = (f32[256,8]{0,1:T(8,128)S(1)}, f32[256,8]{0,1:T(8,128)S(1)}, u32[]{:S(2)}, u32[]{:S(2)}) collective-permute-start(f32[256,8]{0,1:T(8,128)S(1)} %get-tuple-element.53), channel_id=1, source_target_pairs={{0,8},{8,16},{16,24},{1,9},{9,17},{17,25},{2,10},{10,18},{18,26},{... | collective-permute-start | bytes 24584 | tf_op jit(solution)/shard_map/ppermute | solution.py:13
  200.6 10.4 %collective-permute-start.8 = (f32[256,8]{0,1:T(8,128)S(1)}, f32[256,8]{0,1:T(8,128)S(1)}, u32[]{:S(2)}, u32[]{:S(2)}) collective-permute-start(f32[256,8]{0,1:T(8,128)S(1)} %get-tuple-element.51), channel_id=1, source_target_pairs={{0,1},{1,2},{2,3},{3,4},{4,5},{5,6},{6,7},{8,9},{9,10},{10,11},{11... | collective-permute-start | bytes 24584 | tf_op jit(solution)/shard_map/ppermute | solution.py:13
  206.0 6.2 %collective-permute-start.11 = (f32[256,8]{0,1:T(8,128)S(1)}, f32[256,8]{0,1:T(8,128)S(1)}, u32[]{:S(2)}, u32[]{:S(2)}) collective-permute-start(f32[256,8]{0,1:T(8,128)S(1)} %copy.119), channel_id=1, source_target_pairs={{8,0},{16,8},{24,16},{9,1},{17,9},{25,17},{10,2},{18,10},{26,18},{... | collective-permute-start | bytes 24584 | tf_op jit(solution)/shard_map/ppermute | solution.py:13
  208.7 3.7 %collective-permute-start.9 = (f32[256,8]{0,1:T(8,128)S(1)}, f32[256,8]{0,1:T(8,128)S(1)}, u32[]{:S(2)}, u32[]{:S(2)}) collective-permute-start(f32[256,8]{0,1:T(8,128)S(1)} %copy.115), channel_id=1, source_target_pairs={{1,0},{2,1},{3,2},{4,3},{5,4},{6,5},{7,6},{9,8},{10,9},{11,10},{12... | collective-permute-start | bytes 24584 | tf_op jit(solution)/shard_map/ppermute | solution.py:13
